TPU v7x, 32 devices: a whole 2x2x4 slice. The times are simulated.
32 devices in a mesh: rx: 4 (over y, x), chirp: 8 (over z, core).
Axes of the slice: x: 2, y: 2, z: 4, core: 2. Of those that a mesh axis runs over, the one named last changes fastest.
Arguments:
- samples: bfloat16 [2, 128, 128, 4096], P(None, None, 'rx', 'chirp'), may hold values from -6 to 6
- tx_offsets: int32 [12], replicated, may hold values from 0 to 3840, as said below
- band_owner: int32 [16], replicated, may hold values from 0 to 3, as said below
- beam_weights: bfloat16 [2, 256, 1536], replicated, may hold values from -0.109375 to 0.109375
Outputs:
- tile_store: bfloat16 [48, 2, 256, 2048], P('rx', None, None, 'chirp')
Inputs may be any that keep to these rules, and one draw needn't show every extreme that they name: `tx_offsets`: each offset is 256 times a Doppler slot of 0 to 15; transmitters use different slots, and slots 0 and 15 are always used. `band_owner`: at most 12 bands share an owner, and one owner has exactly 12.
All inputs are finite; a program needn't handle non-finite values.
Results may differ from a plain program's by a relative error of at most 0.007.
Values may be sent and summed in bfloat16 or wider, within the bound.
No kernel may reach another device: no remote copies, remote signals or barrier semaphores. Data moves between devices by JAX's collectives and lax.ppermute only.
A program may use at most 192 MiB of HBM per device.

v0:
```python
from functools import partial
import math
import jax
import jax.numpy as jnp
from jax import lax
from jax.sharding import PartitionSpec as P

K1 = 64
K2 = 64
SLOTS = 16


def dft_pair(size):
    indices = jnp.arange(size, dtype=jnp.int32)
    product = indices[:, None] * indices[None, :] % size
    phase_angle = product.astype(jnp.float32) * (-2.0 * math.pi / size)
    scale = 1.0 / math.sqrt(size)
    return (
        (jnp.cos(phase_angle) * scale).astype(jnp.bfloat16),
        (jnp.sin(phase_angle) * scale).astype(jnp.bfloat16),
    )


def twiddle_table():
    outer = jnp.arange(K1, dtype=jnp.int32)[:, None]
    inner = jnp.arange(K2, dtype=jnp.int32)[None, :]
    phase_angle = (outer * inner % (K1 * K2)).astype(jnp.float32) * (-2.0 * math.pi / (K1 * K2))
    return (jnp.cos(phase_angle), jnp.sin(phase_angle))


def spectrum_of(real_part, imag_part, row_count):
    mixing = partial(jnp.einsum, preferred_element_type=jnp.float32)
    split_re = real_part.reshape(row_count, K1, K2)
    split_im = imag_part.reshape(row_count, K1, K2)
    table_re, table_im = dft_pair(K1)
    section_re = mixing("kn,rnm->rkm", table_re, split_re) - mixing(
        "kn,rnm->rkm", table_im, split_im
    )
    section_im = mixing("kn,rnm->rkm", table_re, split_im) + mixing(
        "kn,rnm->rkm", table_im, split_re
    )
    twist_re, twist_im = twiddle_table()
    turned_re = (section_re * twist_re - section_im * twist_im).astype(jnp.bfloat16)
    turned_im = (section_re * twist_im + section_im * twist_re).astype(jnp.bfloat16)
    final_re, final_im = dft_pair(K2)
    out_re = mixing("qm,rkm->rqk", final_re, turned_re) - mixing("qm,rkm->rqk", final_im, turned_im)
    out_im = mixing("qm,rkm->rqk", final_re, turned_im) + mixing("qm,rkm->rqk", final_im, turned_re)
    return (
        out_re.reshape(row_count, K1 * K2).astype(jnp.bfloat16),
        out_im.reshape(row_count, K1 * K2).astype(jnp.bfloat16),
    )


def shards(samples, tx_offsets, band_owner, beam_weights):
    owners = lax.axis_size("rx")
    band_count = band_owner.shape[0]
    capacity = 3 * band_count // owners
    tx_count = tx_offsets.shape[0]
    bin_count = K1 * K2
    speed_bins = bin_count // SLOTS
    band_width = speed_bins // band_count
    starts = (tx_offsets - speed_bins // 2) % bin_count
    sender = jnp.arange(tx_count, dtype=jnp.int32)[:, None]
    speed = jnp.arange(speed_bins, dtype=jnp.int32)[None, :] - speed_bins // 2
    phase_angle = (sender * speed).astype(jnp.float32) * (-2.0 * math.pi / (tx_count * speed_bins))
    cos_part = jnp.cos(phase_angle)[:, None, None, :]
    sin_part = jnp.sin(phase_angle)[:, None, None, :]
    pieces = lax.all_to_all(samples, "chirp", split_axis=1, concat_axis=3, tiled=True)
    bin_rows = pieces.shape[1]
    item_count = pieces.shape[2]
    spec_re, spec_im = spectrum_of(
        pieces[0].reshape(bin_rows * item_count, bin_count),
        pieces[1].reshape(bin_rows * item_count, bin_count),
        bin_rows * item_count,
    )
    joined = jnp.stack([spec_re, spec_im]).reshape(2, bin_rows, item_count, bin_count)
    double = jnp.concatenate([joined, joined], axis=3)

    def take_band(begin_at):
        return lax.dynamic_slice_in_dim(double, begin_at, speed_bins, 3)

    picked = jax.vmap(take_band)(starts)
    got_re = picked[:, 0].astype(jnp.float32)
    got_im = picked[:, 1].astype(jnp.float32)
    demux_re = got_re * cos_part - got_im * sin_part
    demux_im = got_re * sin_part + got_im * cos_part
    demuxed = jnp.stack([demux_re, demux_im]).astype(jnp.bfloat16)
    demuxed = demuxed.transpose(0, 1, 3, 2, 4)
    rx_local = demuxed.shape[2]
    bin_rows = demuxed.shape[3]
    tile_width = bin_rows * band_width
    tiles = demuxed.reshape(2, tx_count, rx_local, bin_rows, band_count, band_width)
    tiles = tiles.transpose(4, 0, 1, 2, 3, 5).reshape(band_count, 2, tx_count, rx_local, tile_width)
    counter = jnp.arange(band_count, dtype=jnp.int32)
    same_owner = band_owner[:, None] == band_owner[None, :]
    earlier = counter[None, :] < counter[:, None]
    band_rank = jnp.sum((same_owner & earlier).astype(jnp.int32), axis=1)
    weight_re = beam_weights[0]
    weight_im = beam_weights[1]
    slot_ids = band_owner * capacity + band_rank
    choose = (slot_ids[None, :] == jnp.arange(owners * capacity, dtype=jnp.int32)[:, None]).astype(
        jnp.bfloat16
    )
    outgoing = jnp.dot(
        choose, tiles.reshape(band_count, -1), preferred_element_type=jnp.float32
    ).astype(jnp.bfloat16)
    outgoing = outgoing.reshape(owners, capacity, 2, tx_count, rx_local, tile_width)
    slots = lax.all_to_all(outgoing, "rx", split_axis=0, concat_axis=4, tiled=True)[0]
    item_count = slots.shape[0]
    channels = slots.reshape(item_count, 2, slots.shape[2] * slots.shape[3], slots.shape[4])
    mixing = partial(jnp.einsum, preferred_element_type=jnp.float32)
    beam_re = mixing("bc,scm->sbm", weight_re, channels[:, 0]) - mixing(
        "bc,scm->sbm", weight_im, channels[:, 1]
    )
    beam_im = mixing("bc,scm->sbm", weight_re, channels[:, 1]) + mixing(
        "bc,scm->sbm", weight_im, channels[:, 0]
    )
    return jnp.stack([beam_re, beam_im], axis=1).astype(jnp.bfloat16)


def solution(mesh):
    placed = (P(None, None, "rx", "chirp"), P(), P(), P())
    return jax.shard_map(
        shards, mesh=mesh, in_specs=placed, out_specs=P("rx", None, None, "chirp"), check_vma=False
    )
```

profile of v0, /device:TPU:0, one launch (start us, length us, event | category | flops | bytes accessed | tf_op | source)
XLA Modules:
  0.0 832.5 jit_solution(5319038525160731027)
XLA Ops:
  0.0 8.3 copy.56
  8.3 6.5 all-to-all-start
  15.7 183.0 %all-to-all-done = bf16[2,128,32,512]{3,2,0,1:T(8,128)(2,1)} async-done(((bf16[2,128,32,512]{3,2,0,1:T(8,128)(2,1)}), bf16[2,128,32,512]{3,2,0,1:T(8,128)(2,1)}, u32[]{:S(2)}, u32[]{:S(2)}) %all-to-all-start) | async-done | bytes 8388640 | tf_op jit(solution)/shard_map/all_to_all | solution.py:68
  198.7 15.4 %copy.96 = bf16[2,8,16,32,512]{4,1,3,2,0:T(8,128)(2,1)} copy(bf16[2,8,16,32,512]{4,3,0,2,1:T(8,128)(2,1)} %bitcast.1) | data formatting | bytes 16777216 | tf_op jit(solution)/shard_map/all_to_all | solution.py:68
  214.1 5.9 fusion.107
  220.0 11.2 %reshape_reshape_squeeze.7 = bf16[512,64,64]{2,1,0:T(8,128)(2,1)} reshape(bf16[1,16,32,8,512]{4,3,2,1,0:T(8,128)(2,1)} %get-tuple-element.24) | data formatting | bytes 8388608 | tf_op jit(solution)/shard_map/reshape;reshape;squeeze | solution.py:34
  231.2 12.2 %copy.59 = bf16[512,64,64]{0,1,2:T(8,128)(2,1)} copy(bf16[512,64,64]{2,1,0:T(8,128)(2,1)} %reshape_reshape_squeeze.7) | data formatting | bytes 8388608 | tf_op jit(solution)/shard_map/reshape;reshape;squeeze | solution.py:34
  243.4 6.9 fusion.55
  250.3 4.6 fusion.59
  254.9 11.2 %reshape_reshape_squeeze.6 = bf16[512,64,64]{2,1,0:T(8,128)(2,1)} reshape(bf16[1,16,32,8,512]{4,3,2,1,0:T(8,128)(2,1)} %get-tuple-element.23) | data formatting | bytes 8388608 | tf_op jit(solution)/shard_map/reshape;reshape;squeeze | solution.py:33
  266.1 12.0 %copy.58 = bf16[512,64,64]{0,1,2:T(8,128)(2,1)} copy(bf16[512,64,64]{2,1,0:T(8,128)(2,1)} %reshape_reshape_squeeze.6) | data formatting | bytes 8388608 | tf_op jit(solution)/shard_map/reshape;reshape;squeeze | solution.py:33
  278.1 6.9 fusion.53
  285.0 12.4 %fusion.8 = (bf16[512,64,64]{0,1,2:T(8,128)(2,1)}, bf16[512,64,64]{0,1,2:T(8,128)(2,1)S(1)}) fusion(f32[64,64]{0,1:T(8,128)S(1)} %copy.63, f32[64,64]{0,1:T(8,128)S(1)} %copy.60, f32[64,512,64]{1,0,2:T(8,128)} %fusion.59, f32[64,512,64]{1,0,2:T(8,128)} %fusion.53, f32[64,512,64]{1,0,2:T(8,128)} %fusion.55, bf16[512,64,64]{0,1,2:T(8,128)(2,1)S(1)} %copy-done), kind=kOutput, calls=%fused_computation.24 | convolution fusion | flops 289472512 | bytes 37781504 | tf_op jit(solution)/shard_map/kn,rnm->rkm/dot_general | solution.py:36
  297.4 5.6 fusion.12
  303.0 8.8 %fusion.14 = f32[512,64,64]{0,2,1:T(8,128)} fusion(bf16[512,64,64]{0,1,2:T(8,128)(2,1)S(1)} %get-tuple-element.22), kind=kOutput, calls=%fused_computation.30 | convolution fusion | flops 268500992 | bytes 12582912 | tf_op jit(solution)/shard_map/qm,rkm->rqk/dot_general | solution.py:47
  311.8 8.1 fusion.10
  319.9 15.6 %copy.66 = bf16[512,64,64]{2,1,0:T(8,128)(2,1)} copy(bf16[512,64,64]{0,1,2:T(8,128)(2,1)} %fusion.10) | data formatting | bytes 8388608 | tf_op jit(solution)/shard_map/convert_element_type | solution.py:49
  335.5 12.0 %convert_element_type.170 = bf16[1,16,32,4096]{3,2,1,0:T(8,128)(2,1)} reshape(bf16[512,64,64]{2,1,0:T(8,128)(2,1)} %copy.66) | data formatting | bytes 8388608 | tf_op jit(solution)/shard_map/convert_element_type | solution.py:49
  347.6 12.4 %fusion.11 = bf16[512,64,64]{0,1,2:T(8,128)(2,1)} fusion(f32[512,64,64]{0,2,1:T(8,128)} %fusion.14, bf16[512,64,64]{0,1,2:T(8,128)(2,1)} %get-tuple-element.21), kind=kOutput, calls=%fused_computation.27 | convolution fusion | flops 272695296 | bytes 16777216 | tf_op jit(solution)/shard_map/qm,rkm->rqk/dot_general | solution.py:47
  359.9 15.8 %copy.69 = bf16[512,64,64]{2,1,0:T(8,128)(2,1)} copy(bf16[512,64,64]{0,1,2:T(8,128)(2,1)} %fusion.11) | data formatting | bytes 8388608 | tf_op jit(solution)/shard_map/convert_element_type | solution.py:50
  375.7 12.1 %convert_element_type.173 = bf16[1,16,32,4096]{3,2,1,0:T(8,128)(2,1)} reshape(bf16[512,64,64]{2,1,0:T(8,128)(2,1)} %copy.69) | data formatting | bytes 8388608 | tf_op jit(solution)/shard_map/convert_element_type | solution.py:50
  387.8 14.0 %maximum_maximum_fusion = bf16[2,16,32,8192]{3,2,1,0:T(8,128)(2,1)} fusion(bf16[1,16,32,4096]{3,2,1,0:T(8,128)(2,1)} %convert_element_type.173, bf16[1,16,32,4096]{3,2,1,0:T(8,128)(2,1)} %convert_element_type.170), kind=kLoop, calls=%fused_computation.3 | loop fusion | flops 67108864 | bytes 25165824 | tf_op jit(solution)/shard_map/concatenate | solution.py:77
  401.8 41.0 %while.1 = (s32[]{:T(128)}, bf16[2,16,32,8192]{3,2,1,0:T(8,128)(2,1)}, s32[12,4]{0,1:T(4,128)S(1)}, bf16[12,2,16,32,256]{4,3,2,0,1:T(8,128)(2,1)}, s32[]{:T(128)}) while((s32[]{:T(128)}, bf16[2,16,32,8192]{3,2,1,0:T(8,128)(2,1)}, s32[12,4]{0,1:T(4,128)S(1)}, bf16[12,2,16,32,256]{4,3,2,0,1:T(8,128)(2,1)}, s32[]{:T(128)}) %tuple.20), condition=%wide.while_cond, body=%wide.while_body.sunk | while | flops 2 | bytes 1049705 | solution.py:80
  450.0 21.0 %copy.72 = bf16[2,12,16,32,256]{3,4,2,1,0:T(8,128)(2,1)} copy(bf16[2,12,16,32,256]{4,3,2,1,0:T(8,128)(2,1)} %pad_maximum_fusion) | data formatting | bytes 12582912 | tf_op jit(solution)/shard_map/stack | solution.py:87
  471.0 54.6 %copy.73 = bf16[16,2,12,32,16,16]{5,4,3,2,1,0:T(8,128)(2,1)} copy(bf16[16,2,12,32,16,16]{3,5,0,4,2,1:T(8,128)(2,1)} %bitcast.110) | data formatting | bytes 12582912 | tf_op jit(solution)/shard_map/transpose | solution.py:93
  525.6 45.0 %reshape_reshape.3 = bf16[16,196608]{1,0:T(8,128)(2,1)} reshape(bf16[16,2,12,32,16,16]{5,4,3,2,1,0:T(8,128)(2,1)} %copy.73) | data formatting | bytes 12582912 | tf_op jit(solution)/shard_map/reshape;reshape | solution.py:105
  570.6 11.8 %convolution_convert_fusion = bf16[48,196608]{1,0:T(8,128)(2,1)} fusion(bf16[16,196608]{1,0:T(8,128)(2,1)} %reshape_reshape.3, s32[16]{0:T(128)S(1)} %multiply_add_fusion), kind=kOutput, calls=%fused_computation.2 | convolution fusion | flops 311427840 | bytes 25165888 | tf_op jit(solution)/shard_map/dot_general | solution.py:104
  582.5 11.5 %copy.82 = bf16[6,8,768,256]{3,2,1,0:T(8,128)(2,1)S(1)} copy(bf16[6,8,768,256]{3,1,2,0:T(8,128)(2,1)} %bitcast.111) | data formatting | bytes 37748736
  593.9 208.6 %all_to_all.30 = bf16[4,12,2,12,32,256]{5,4,3,2,1,0:T(8,128)(2,1)S(1)} all-to-all(bf16[4,12,2,12,32,256]{5,4,3,2,1,0:T(8,128)(2,1)S(1)} %bitcast.112), channel_id=1, replica_groups=mesh['rx'=4,'chirp'=8] {'rx'}, dimensions={0} | all-to-all | bytes 37748736 | tf_op jit(solution)/shard_map/all_to_all | solution.py:108
  802.5 6.6 copy.74
  809.1 8.2 fusion.1
  822.0 4.4 fusion.24
  (69 shorter events, 59.5 us)
Async XLA Ops:
  8.3 7.0 copy-start.6
  8.3 7.2 copy-start.5
  8.3 190.4 %all-to-all-start = ((bf16[2,128,32,512]{3,2,0,1:T(8,128)(2,1)}), bf16[2,128,32,512]{3,2,0,1:T(8,128)(2,1)}, u32[]{:S(2)}, u32[]{:S(2)}) async-start(bf16[2,128,32,512]{3,2,0,1:T(8,128)(2,1)} %copy.56), calls=%async_computation | async-start | bytes 16777216 | tf_op jit(solution)/shard_map/all_to_all | solution.py:68
  243.3 6.9 copy-start.1
  278.1 6.9 copy-start
  303.0 8.8 %copy-start.2 = (bf16[512,64,64]{0,1,2:T(8,128)(2,1)S(1)}, bf16[512,64,64]{0,1,2:T(8,128)(2,1)}, u32[]{:S(2)}) copy-start(bf16[512,64,64]{0,1,2:T(8,128)(2,1)} %get-tuple-element.21) | copy-start | bytes 12582916
  802.5 6.6 copy-start.4
  809.1 10.2 %copy-start.3 = (bf16[4,12,2,12,32,256]{5,4,0,3,2,1:T(8,128)(2,1)S(1)}, bf16[4,12,2,12,32,256]{5,4,0,3,2,1:T(8,128)(2,1)}, u32[]{:S(2)}) copy-start(bf16[4,12,2,12,32,256]{5,4,0,3,2,1:T(8,128)(2,1)} %copy.74) | copy-start | bytes 56623108
where the time goes:
time: 846 us; the launch traced here: 832 us
  local copies, waits for them, and re-layouts  316 us (37%)
  blocking collectives  209 us (25%)
  waiting for transfers between devices  183 us (22%)
  matrix products  95.3 us (11%)
  other arithmetic  22.2 us (3%)
    all_to_all x1, blocking collectives, shards(): lax.all_to_all(outgoing, 'rx', split_axis=0, concat_axis=4, tiled=True)[0]  209 us
    all_to_all x1, waiting for transfers between devices, shards(): lax.all_to_all(samples, 'chirp', split_axis=1, concat_axis=3, tiled=True)  183 us
    transpose x1, local copies, waits for them, and re-layouts, shards(): tiles.transpose(4, 0, 1, 2, 3, 5)  54.6 us
    another operation x1, local copies, waits for them, and re-layouts, shards(): tiles.reshape(band_count, -1)  45 us
    gather x36, local copies, waits for them, and re-layouts  41 us
    convert_element_type x2, local copies, waits for them, and re-layouts, spectrum_of(): out_im.reshape(row_count, K1 * K2).astype(jnp.bfloat16)  27.9 us
    convert_element_type x2, local copies, waits for them, and re-layouts, spectrum_of(): out_re.reshape(row_count, K1 * K2).astype(jnp.bfloat16)  27.7 us
    another operation x2, local copies, waits for them, and re-layouts, spectrum_of(): split_im = imag_part.reshape(row_count, K1, K2)  23.4 us
  transfers between devices with their start and end apart: 1, of which 1 were waited for; matrix products, arithmetic and copies ran while one was open for 0% of the time, Pallas kernels for 0%

commit v1 on v0

--- a/solution.py
+++ b/solution.py
@@ -1,3 +1,4 @@
+import functools
 from functools import partial
 import math
 import jax
@@ -8,6 +9,22 @@
 K1 = 64
 K2 = 64
 SLOTS = 16
+
+
+def joints_pack(panel, dim_i, dim_no):
+    known = jnp.concatenate(
+        lax.all_to_all(
+            jnp.stack(jnp.split(panel, lax.axis_size("chirp"), axis=dim_i), axis=0),
+            axis_name="chirp",
+            split_axis=0,
+            concat_axis=0,
+        ),
+        axis=dim_no,
+    )
+    return known
+
+
+local_data_measure = functools.partial(joints_pack, dim_i=1, dim_no=3)
 
 
 def dft_pair(size):
@@ -65,7 +82,7 @@
     phase_angle = (sender * speed).astype(jnp.float32) * (-2.0 * math.pi / (tx_count * speed_bins))
     cos_part = jnp.cos(phase_angle)[:, None, None, :]
     sin_part = jnp.sin(phase_angle)[:, None, None, :]
-    pieces = lax.all_to_all(samples, "chirp", split_axis=1, concat_axis=3, tiled=True)
+    pieces = local_data_measure(samples)
     bin_rows = pieces.shape[1]
     item_count = pieces.shape[2]
     spec_re, spec_im = spectrum_of(

time: 846 us -> 851 us (level)
    all_to_all x1 -> x0, local copies, waits for them, and re-layouts: 15.4 us -> none  [shards(): lax.all_to_all(samples, 'chirp', split_axis=1, concat_axis=3, tiled=True)]
    unnamed x16 -> x24, local copies, waits for them, and re-layouts: 21.8 us -> 29.9 us
where the time goes in v1:
time: 851 us; the launch traced here: 837 us
  local copies, waits for them, and re-layouts  321 us (38%)
  blocking collectives  209 us (25%)
  waiting for transfers between devices  183 us (22%)
  matrix products  95.1 us (11%)
  other arithmetic  22.2 us (3%)
    all_to_all x1, blocking collectives, shards(): lax.all_to_all(outgoing, 'rx', split_axis=0, concat_axis=4, tiled=True)[0]  209 us
    all_to_all x1, waiting for transfers between devices, joints_pack(): lax.all_to_all(jnp.stack(jnp.split(panel, lax.axis_size('chirp'), axis=di...  183 us
    transpose x1, local copies, waits for them, and re-layouts, shards(): tiles.transpose(4, 0, 1, 2, 3, 5)  54.6 us
    another operation x1, local copies, waits for them, and re-layouts, shards(): tiles.reshape(band_count, -1)  45 us
    gather x36, local copies, waits for them, and re-layouts  41.5 us
    unnamed x24, local copies, waits for them, and re-layouts  29.9 us
    convert_element_type x2, local copies, waits for them, and re-layouts, spectrum_of(): out_im.reshape(row_count, K1 * K2).astype(jnp.bfloat16)  27.9 us
    convert_element_type x2, local copies, waits for them, and re-layouts, spectrum_of(): out_re.reshape(row_count, K1 * K2).astype(jnp.bfloat16)  27.7 us
  transfers between devices with their start and end apart: 1, of which 1 were waited for; matrix products, arithmetic and copies ran while one was open for 0% of the time, Pallas kernels for 0%

profile of v1, /device:TPU:0, one launch (start us, length us, event | category | flops | bytes accessed | tf_op | source)
XLA Modules:
  0.0 837.0 jit_solution(191411274853438230)
XLA Ops:
  18.7 6.5 all-to-all-start
  26.1 183.0 %all-to-all-done = bf16[8,2,16,32,512]{4,3,2,1,0:T(8,128)(2,1)} async-done(((bf16[8,2,16,32,512]{4,3,2,1,0:T(8,128)(2,1)}), bf16[8,2,16,32,512]{4,3,2,1,0:T(8,128)(2,1)}, u32[]{:S(2)}, u32[]{:S(2)}) %all-to-all-start) | async-done | bytes 8388640 | tf_op jit(solution)/shard_map/all_to_all | solution.py:16
  209.1 5.3 fusion.109
  214.5 4.9 copy.57
  219.3 11.2 %reshape_reshape_squeeze.6 = bf16[512,64,64]{2,1,0:T(8,128)(2,1)} reshape(bf16[1,16,32,8,512]{4,3,2,1,0:T(8,128)(2,1)} %copy.57) | data formatting | bytes 8388608 | tf_op jit(solution)/shard_map/reshape;reshape;squeeze | solution.py:50
  230.5 12.1 %copy.58 = bf16[512,64,64]{0,1,2:T(8,128)(2,1)} copy(bf16[512,64,64]{2,1,0:T(8,128)(2,1)} %reshape_reshape_squeeze.6) | data formatting | bytes 8388608 | tf_op jit(solution)/shard_map/reshape;reshape;squeeze | solution.py:50
  242.6 6.9 fusion.55
  249.5 4.6 fusion.59
  254.1 4.9 copy.59
  259.0 11.2 %reshape_reshape_squeeze.7 = bf16[512,64,64]{2,1,0:T(8,128)(2,1)} reshape(bf16[1,16,32,8,512]{4,3,2,1,0:T(8,128)(2,1)} %copy.59) | data formatting | bytes 8388608 | tf_op jit(solution)/shard_map/reshape;reshape;squeeze | solution.py:51
  270.2 12.2 %copy.60 = bf16[512,64,64]{0,1,2:T(8,128)(2,1)} copy(bf16[512,64,64]{2,1,0:T(8,128)(2,1)} %reshape_reshape_squeeze.7) | data formatting | bytes 8388608 | tf_op jit(solution)/shard_map/reshape;reshape;squeeze | solution.py:51
  282.3 6.9 fusion.53
  289.2 12.3 %fusion.1 = (bf16[512,64,64]{0,1,2:T(8,128)(2,1)}, bf16[512,64,64]{0,1,2:T(8,128)(2,1)S(1)}) fusion(f32[64,64]{0,1:T(8,128)S(1)} %copy.64, f32[64,64]{0,1:T(8,128)S(1)} %copy.61, f32[512,64,64]{0,2,1:T(8,128)} %fusion.55, f32[512,64,64]{0,2,1:T(8,128)} %fusion.59, f32[512,64,64]{0,2,1:T(8,128)} %fusion.53, bf16[512,64,64]{0,1,2:T(8,128)(2,1)S(1)} %copy-done), kind=kOutput, calls=%fused_computation.9 | convolution fusion | flops 289472512 | bytes 37781504 | tf_op jit(solution)/shard_map/kn,rnm->rkm/dot_general | solution.py:56
  301.5 5.6 fusion.14
  307.1 8.8 %fusion.16 = f32[512,64,64]{0,2,1:T(8,128)} fusion(bf16[512,64,64]{0,1,2:T(8,128)(2,1)S(1)} %get-tuple-element.22), kind=kOutput, calls=%fused_computation.33 | convolution fusion | flops 268500992 | bytes 12582912 | tf_op jit(solution)/shard_map/qm,rkm->rqk/dot_general | solution.py:64
  315.9 8.1 fusion.12
  323.9 15.6 %copy.67 = bf16[512,64,64]{2,1,0:T(8,128)(2,1)} copy(bf16[512,64,64]{0,1,2:T(8,128)(2,1)} %fusion.12) | data formatting | bytes 8388608 | tf_op jit(solution)/shard_map/convert_element_type | solution.py:66
  339.6 12.0 %convert_element_type.162 = bf16[1,16,32,4096]{3,2,1,0:T(8,128)(2,1)} reshape(bf16[512,64,64]{2,1,0:T(8,128)(2,1)} %copy.67) | data formatting | bytes 8388608 | tf_op jit(solution)/shard_map/convert_element_type | solution.py:66
  351.6 12.3 %fusion.13 = bf16[512,64,64]{0,1,2:T(8,128)(2,1)} fusion(f32[512,64,64]{0,2,1:T(8,128)} %fusion.16, bf16[512,64,64]{0,1,2:T(8,128)(2,1)} %get-tuple-element.21), kind=kOutput, calls=%fused_computation.30 | convolution fusion | flops 272695296 | bytes 16777216 | tf_op jit(solution)/shard_map/qm,rkm->rqk/dot_general | solution.py:64
  364.0 15.8 %copy.70 = bf16[512,64,64]{2,1,0:T(8,128)(2,1)} copy(bf16[512,64,64]{0,1,2:T(8,128)(2,1)} %fusion.13) | data formatting | bytes 8388608 | tf_op jit(solution)/shard_map/convert_element_type | solution.py:67
  379.8 12.1 %convert_element_type.165 = bf16[1,16,32,4096]{3,2,1,0:T(8,128)(2,1)} reshape(bf16[512,64,64]{2,1,0:T(8,128)(2,1)} %copy.70) | data formatting | bytes 8388608 | tf_op jit(solution)/shard_map/convert_element_type | solution.py:67
  391.9 14.0 %maximum_maximum_fusion = bf16[2,16,32,8192]{3,2,1,0:T(8,128)(2,1)} fusion(bf16[1,16,32,4096]{3,2,1,0:T(8,128)(2,1)} %convert_element_type.165, bf16[1,16,32,4096]{3,2,1,0:T(8,128)(2,1)} %convert_element_type.162), kind=kLoop, calls=%fused_computation.3 | loop fusion | flops 67108864 | bytes 25165824 | tf_op jit(solution)/shard_map/concatenate | solution.py:94
  405.8 41.5 %while.1 = (s32[]{:T(128)}, bf16[2,16,32,8192]{3,2,1,0:T(8,128)(2,1)}, s32[12,4]{0,1:T(4,128)S(1)}, bf16[12,2,16,32,256]{4,3,2,0,1:T(8,128)(2,1)}, s32[]{:T(128)}) while((s32[]{:T(128)}, bf16[2,16,32,8192]{3,2,1,0:T(8,128)(2,1)}, s32[12,4]{0,1:T(4,128)S(1)}, bf16[12,2,16,32,256]{4,3,2,0,1:T(8,128)(2,1)}, s32[]{:T(128)}) %tuple.20), condition=%wide.while_cond, body=%wide.while_body.sunk | while | flops 2 | bytes 1049705 | solution.py:97
  454.6 21.0 %copy.73 = bf16[2,12,16,32,256]{3,4,2,1,0:T(8,128)(2,1)} copy(bf16[2,12,16,32,256]{4,3,2,1,0:T(8,128)(2,1)} %pad_maximum_fusion) | data formatting | bytes 12582912 | tf_op jit(solution)/shard_map/stack | solution.py:104
  475.6 54.6 %copy.74 = bf16[16,2,12,32,16,16]{5,4,3,2,1,0:T(8,128)(2,1)} copy(bf16[16,2,12,32,16,16]{3,5,0,4,2,1:T(8,128)(2,1)} %bitcast.137) | data formatting | bytes 12582912 | tf_op jit(solution)/shard_map/transpose | solution.py:110
  530.1 45.0 %reshape_reshape.3 = bf16[16,196608]{1,0:T(8,128)(2,1)} reshape(bf16[16,2,12,32,16,16]{5,4,3,2,1,0:T(8,128)(2,1)} %copy.74) | data formatting | bytes 12582912 | tf_op jit(solution)/shard_map/reshape;reshape | solution.py:122
  575.1 11.8 %convolution_convert_fusion = bf16[48,196608]{1,0:T(8,128)(2,1)} fusion(bf16[16,196608]{1,0:T(8,128)(2,1)} %reshape_reshape.3, s32[16]{0:T(128)S(1)} %multiply_add_fusion), kind=kOutput, calls=%fused_computation.2 | convolution fusion | flops 311427840 | bytes 25165888 | tf_op jit(solution)/shard_map/dot_general | solution.py:121
  587.0 11.5 %copy.83 = bf16[6,8,768,256]{3,2,1,0:T(8,128)(2,1)S(1)} copy(bf16[6,8,768,256]{3,1,2,0:T(8,128)(2,1)} %bitcast.138) | data formatting | bytes 37748736
  598.4 208.6 %all_to_all.20 = bf16[4,12,2,12,32,256]{5,4,3,2,1,0:T(8,128)(2,1)S(1)} all-to-all(bf16[4,12,2,12,32,256]{5,4,3,2,1,0:T(8,128)(2,1)S(1)} %bitcast.139), channel_id=1, replica_groups=mesh['rx'=4,'chirp'=8] {'rx'}, dimensions={0} | all-to-all | bytes 37748736 | tf_op jit(solution)/shard_map/all_to_all | solution.py:125
  807.0 6.6 copy.75
  813.6 8.2 fusion.5
  826.5 4.4 fusion.26
  (79 shorter events, 78.7 us)
Async XLA Ops:
  18.7 7.0 copy-start.7
  18.7 7.2 copy-start.6
  18.7 190.4 %all-to-all-start = ((bf16[8,2,16,32,512]{4,3,2,1,0:T(8,128)(2,1)}), bf16[8,2,16,32,512]{4,3,2,1,0:T(8,128)(2,1)}, u32[]{:S(2)}, u32[]{:S(2)}) async-start(bf16[8,2,16,32,512]{4,3,2,1,0:T(8,128)(2,1)} %bitcast_dynamic-update-slice_fusion.1), calls=%async_computation | async-start | bytes 16777216 | tf_op jit(solution)/shard_map/all_to_all | solution.py:16
  242.6 6.9 copy-start.1
  249.5 4.6 copy-start.4
  282.3 6.9 copy-start
  307.1 8.8 %copy-start.2 = (bf16[512,64,64]{0,1,2:T(8,128)(2,1)S(1)}, bf16[512,64,64]{0,1,2:T(8,128)(2,1)}, u32[]{:S(2)}) copy-start(bf16[512,64,64]{0,1,2:T(8,128)(2,1)} %get-tuple-element.21) | copy-start | bytes 12582916
  807.0 6.6 copy-start.5
  813.6 10.2 %copy-start.3 = (bf16[4,12,2,12,32,256]{5,4,0,3,2,1:T(8,128)(2,1)S(1)}, bf16[4,12,2,12,32,256]{5,4,0,3,2,1:T(8,128)(2,1)}, u32[]{:S(2)}) copy-start(bf16[4,12,2,12,32,256]{5,4,0,3,2,1:T(8,128)(2,1)} %copy.75) | copy-start | bytes 56623108
